TPU v7x, 32 devices: a whole 2x2x4 slice. The times are simulated.
32 devices in a mesh: row: 8 (over y, x, core), col: 4 (over z).
Axes of the slice: x: 2, y: 2, z: 4, core: 2. Of those that a mesh axis runs over, the one named last changes fastest.
Arguments:
- amplitudes: bfloat16 [4096, 4096], P('row', 'col'), may hold values from -0.1875 to 0.1875
- factors: bfloat16 [4096, 2048], P('col', 'row'), may hold values from -0.125 to 0.125
- tile_map: int32 [16, 16], P('row', 'col'), may hold values 0 or 1
- panel_owner: int32 [2], replicated, may hold values from 0 to 3, as said below
Outputs:
- cycle_term: float32 [4096, 4096], P('row', 'col')
Inputs may be any that keep to these rules, and one draw needn't show every extreme that they name: `panel_owner`: the 2 entries are distinct panel indices, and one of them is the last panel.
All inputs are finite; a program needn't handle non-finite values. No bound on the sum of `tile_map` on one device may be relied on, other than what follows from the above.
Results may differ from a plain program's by a relative error of at most 0.0029.
Values may be sent and summed in bfloat16 or wider, within the bound.
A program may use at most 64 MiB of HBM per device.

v0:
```python
import jax
import jax.numpy as jnp
from jax import lax
from jax.sharding import PartitionSpec as P


def spread(block, axis, owner):
    block = jnp.where(lax.axis_index(axis) == owner, block, jnp.zeros_like(block))
    return lax.psum(block, axis)


def keep_tiles(block, tiles):
    rows, cols = tiles.shape
    shaped = block.reshape(rows, block.shape[0] // rows, cols, block.shape[1] // cols)
    keep = tiles.astype(block.dtype)[:, None, :, None]
    return (shaped * keep).reshape(block.shape)


def outer_rows(left, right):
    return lax.dot_general(
        left, right, (((1,), (1,)), ((), ())), preferred_element_type=jnp.float32
    )


def shards(amplitudes, factors, tile_map, panel_owner):
    kept = keep_tiles(amplitudes, tile_map)
    width = factors.shape[0]
    total = jnp.zeros((kept.shape[0], width), jnp.float32)
    column_factors = lax.all_gather(factors, "row", axis=1, tiled=True)
    for step in range(panel_owner.shape[0]):
        owner = panel_owner[step]
        panel = spread(kept, "col", owner)
        owner_slice = spread(factors, "col", owner)
        owner_factors = lax.all_gather(owner_slice, "row", axis=1, tiled=True)
        integrals = outer_rows(owner_factors, column_factors).astype(jnp.bfloat16)
        total = total + jnp.dot(panel, integrals, preferred_element_type=jnp.float32)
    return keep_tiles(total, tile_map)


def solution(mesh):
    in_specs = (P("row", "col"), P("col", "row"), P("row", "col"), P())
    out_specs = P("row", "col")
    return jax.shard_map(shards, mesh=mesh, in_specs=in_specs, out_specs=out_specs, check_vma=False)
```

profile of v0, /device:TPU:0, one launch (start us, length us, event | category | flops | bytes accessed | tf_op | source)
XLA Modules:
  0.0 232.9 jit_solution(12405336362898462879)
XLA Ops:
  7.4 0.0 all-reduce.3.cloned.1.call-start
  7.4 0.8 fusion.10
  8.2 1.3 fusion.11
  9.4 0.3 mul.22
  9.8 0.2 copy.5
  11.2 2.1 broadcast_select_fusion.3
  13.3 0.0 copy-done
  13.3 1.5 broadcast_select_fusion.1
  14.8 0.0 all-reduce.3.cloned.1.call-update
  14.9 0.0 all-gather.6.cloned.1.call-start
  14.9 0.5 all-gather.6.cloned.1.call-update
  15.4 0.0 all-gather.8.cloned.1.call-start
  15.5 123.3 %all-reduce.3.cloned.1.call-done = (bf16[512,1024]{1,0:T(8,128)(2,1)}, bf16[1024,256]{1,0:T(8,128)(2,1)}, bf16[512,1024]{1,0:T(8,128)(2,1)}, bf16[1024,256]{1,0:T(8,128)(2,1)}) async-done(((bf16[512,1024]{1,0:T(8,128)(2,1)}, bf16[1024,256]{1,0:T(8,128)(2,1)}, bf16[512,1024]{1,0:T(8,128)(2,1)}, bf16[1024,256]{1,0:T(8,128)(2,1)}), (bf16[512,1024]{1,0:T(8,128)(2,1)}, bf16[1024,256]{1,0:T(8,128)(2,1)}, ...) | async-done | bytes 3145744 | tf_op jit(solution)/shard_map/psum | solution.py:9
  138.8 0.0 all-gather.8.cloned.1.call-update
  138.9 0.0 all-gather.4.cloned.1.call-start
  138.9 0.5 all-gather.4.cloned.1.call-update
  139.4 0.3 mul.25
  139.8 0.5 copy.6
  140.3 0.0 all-gather.6.cloned.1.call-done
  140.3 34.9 %all-gather.8.cloned.1.call-done = bf16[1024,2048]{1,0:T(8,128)(2,1)} async-done(((bf16[1024,256]{1,0:T(8,128)(2,1)}), bf16[1024,2048]{1,0:T(8,128)(2,1)}) %all-gather.8.cloned.1.call-update) | async-done | bytes 4194320 | tf_op jit(solution)/shard_map/all_gather | solution.py:34
  175.2 10.8 %fusion = f32[512,1024]{1,0:T(8,128)} fusion(bf16[512,1024]{1,0:T(8,128)(2,1)} %get-tuple-element.5, bf16[1024,2048]{1,0:T(8,128)(2,1)} %all-gather.8.cloned.1.call-done, bf16[1024,2048]{1,0:T(8,128)(2,1)} %all-gather.6.cloned.1.call-done), kind=kOutput, calls=%fused_computation.1 | convolution fusion | flops 5369757696 | bytes 11534336 | tf_op jit(solution)/shard_map/dot_general | solution.py:36
  186.0 28.2 %all-gather.4.cloned.1.call-done = bf16[1024,2048]{1,0:T(8,128)(2,1)} async-done(((bf16[1024,256]{1,0:T(8,128)(2,1)}), bf16[1024,2048]{1,0:T(8,128)(2,1)}) %all-gather.4.cloned.1.call-update) | async-done | bytes 4194320 | tf_op jit(solution)/shard_map/all_gather | solution.py:34
  214.2 0.0 copy-done.1
  214.2 11.1 %add_multiply_fusion = f32[512,1024]{1,0:T(8,128)} fusion(f32[512,1024]{1,0:T(8,128)S(1)} %bitcast.17, f32[512,1024]{1,0:T(8,128)} %fusion, bf16[512,1024]{1,0:T(8,128)(2,1)S(1)} %copy-done.1, bf16[1024,2048]{1,0:T(8,128)(2,1)} %all-gather.4.cloned.1.call-done, bf16[1024,2048]{1,0:T(8,128)(2,1)} %all-gather.6.cloned.1.call-done), kind=kOutput, calls=%fused_computation | convolution fusion | flops 5370806272 | bytes 15728640 | tf_op jit(solution)/shard_map/dot_general | solution.py:36
  (2 shorter events, 0.0 us)
Async XLA Ops:
  7.4 6.0 %copy-start = (bf16[512,1024]{1,0:T(8,128)(2,1)S(1)}, bf16[512,1024]{1,0:T(8,128)(2,1)}, u32[]{:S(2)}) copy-start(bf16[512,1024]{1,0:T(8,128)(2,1)} %param.4) | copy-start | bytes 3145732
  7.4 131.5 %all-reduce.3.cloned.1.call-start = ((), (), s32[]{:S(2)}) async-start(), calls=%async_computation.3 | async-start | bytes 6291456 | tf_op jit(solution)/shard_map/psum | solution.py:9
  14.9 125.4 %all-gather.6.cloned.1.call-start = ((), (), s32[]{:S(2)}) async-start(), calls=%async_computation.1 | async-start | bytes 4718592 | tf_op jit(solution)/shard_map/all_gather | solution.py:29
  15.4 159.8 %all-gather.8.cloned.1.call-start = ((), (), s32[]{:S(2)}) async-start(), calls=%async_computation.2 | async-start | bytes 4718592 | tf_op jit(solution)/shard_map/all_gather | solution.py:34
  138.9 75.3 %all-gather.4.cloned.1.call-start = ((), (), s32[]{:S(2)}) async-start(), calls=%async_computation | async-start | bytes 4718592 | tf_op jit(solution)/shard_map/all_gather | solution.py:34
  175.2 39.0 %copy-start.1 = (bf16[512,1024]{1,0:T(8,128)(2,1)S(1)}, bf16[512,1024]{1,0:T(8,128)(2,1)}, u32[]{:S(2)}) copy-start(bf16[512,1024]{1,0:T(8,128)(2,1)} %get-tuple-element.7) | copy-start | bytes 3145732
Sparse Core Ops, SparseCore 0:
  15.0 123.8 all-reduce.2
Sparse Core Ops, SparseCore 1:
  17.2 39.9 all-gather.5
  139.0 36.2 all-gather.7
  177.0 37.2 all-gather.3
where the time goes:
time: 233 us
  waiting for transfers between devices  188 us (81%)
  matrix products  21.9 us (9%)
  between operations  16.3 us (7%)
  other arithmetic  4.41 us (2%)
  local copies, waits for them, and re-layouts  2.65 us (1%)
    psum x1, waiting for transfers between devices, spread(): return lax.psum(block, axis)  123 us
    all_gather x2, waiting for transfers between devices, shards(): owner_factors = lax.all_gather(owner_slice, 'row', axis=1, tiled=True)  63.1 us
    dot_general x2, matrix products, shards(): jnp.dot(panel, integrals, preferred_element_type=jnp.float32)  21.9 us
  transfers between devices with their start and end apart: 4, of which 3 were waited for; matrix products, arithmetic and copies ran while one was open for 5% of the time, Pallas kernels for 0%

commit v1 on v0

--- a/solution.py
+++ b/solution.py
@@ -31,7 +31,14 @@
         owner = panel_owner[step]
         panel = spread(kept, "col", owner)
         owner_slice = spread(factors, "col", owner)
-        owner_factors = lax.all_gather(owner_slice, "row", axis=1, tiled=True)
+        x = owner_slice
+        ways, here, hop = (lax.axis_size("row"), lax.axis_index("row"), x.shape[1])
+        shape = [n * ways if d == 1 else n for d, n in enumerate(x.shape)]
+        full = lax.dynamic_update_slice_in_dim(jnp.zeros(shape, x.dtype), x, here * hop, axis=1)
+        for far in range(1, ways):
+            x = lax.ppermute(x, "row", [(d, (d + 1) % ways) for d in range(ways)])
+            full = lax.dynamic_update_slice_in_dim(full, x, (here - far) % ways * hop, axis=1)
+        owner_factors = full
         integrals = outer_rows(owner_factors, column_factors).astype(jnp.bfloat16)
         total = total + jnp.dot(panel, integrals, preferred_element_type=jnp.float32)
     return keep_tiles(total, tile_map)

time: 233 us -> 254 us (1.090)
  local copies, waits for them, and re-layouts: 2.65 us -> 26 us
  waiting for transfers between devices: 188 us -> 183 us
    all_gather x2 -> x0, waiting for transfers between devices: 63.1 us -> none  [shards(): owner_factors = lax.all_gather(owner_slice, 'row', axis=1, tiled=True)]
    ppermute x0 -> x14, waiting for transfers between devices: none -> 58.8 us  [shards(): x = lax.ppermute(x, 'row', [(d, (d + 1) % ways) for d in range(ways)])]
    dynamic_update_slice x0 -> x16, local copies, waits for them, and re-layouts: none -> 18.2 us  [the longest x14 16.4 us: shards(): lax.dynamic_update_slice_in_dim(full, x, (here - far) % ways * hop, axis=1)]
    another operation x0 -> x2, local copies, waits for them, and re-layouts: none -> 5.07 us
  transfers between devices with their start and end apart: 4 -> 16, of which waited for: 3 -> 14; matrix products, arithmetic and copies ran while one was open for 5% -> 9% of each run, Pallas kernels for 0% -> 0%
where the time goes in v1:
time: 254 us
  waiting for transfers between devices  183 us (72%)
  local copies, waits for them, and re-layouts  26 us (10%)
  matrix products  22.1 us (9%)
  between operations  16.2 us (6%)
  other arithmetic  4.42 us (2%)
    psum x1, waiting for transfers between devices, spread(): return lax.psum(block, axis)  123 us
    ppermute x14, waiting for transfers between devices, shards(): x = lax.ppermute(x, 'row', [(d, (d + 1) % ways) for d in range(ways)])  58.8 us
    dot_general x2, matrix products, shards(): jnp.dot(panel, integrals, preferred_element_type=jnp.float32)  22.1 us
    dynamic_update_slice x14, local copies, waits for them, and re-layouts, shards(): lax.dynamic_update_slice_in_dim(full, x, (here - far) % ways * hop, axis=1)  16.4 us
  transfers between devices with their start and end apart: 16, of which 14 were waited for; matrix products, arithmetic and copies ran while one was open for 9% of the time, Pallas kernels for 0%

profile of v1, /device:TPU:0, one launch (start us, length us, event | category | flops | bytes accessed | tf_op | source)
XLA Modules:
  0.0 253.8 jit_solution(10970468050443487904)
XLA Ops:
  7.4 1.4 fusion.11
  11.3 2.1 broadcast_select_fusion.3
  13.4 1.6 broadcast_select_fusion.1
  15.6 123.4 %all-reduce.3.cloned.1.call-done = (bf16[512,1024]{1,0:T(8,128)(2,1)}, bf16[1024,256]{1,0:T(8,128)(2,1)}, bf16[512,1024]{1,0:T(8,128)(2,1)}, bf16[1024,256]{1,0:T(8,128)(2,1)}) async-done(((bf16[512,1024]{1,0:T(8,128)(2,1)}, bf16[1024,256]{1,0:T(8,128)(2,1)}, bf16[512,1024]{1,0:T(8,128)(2,1)}, bf16[1024,256]{1,0:T(8,128)(2,1)}), (bf16[512,1024]{1,0:T(8,128)(2,1)}, bf16[1024,256]{1,0:T(8,128)(2,1)}, ...) | async-done | bytes 3145744 | tf_op jit(solution)/shard_map/psum | solution.py:9
  139.0 1.6 collective-permute-start.7
  140.6 8.1 %collective-permute-done = bf16[1024,256]{1,0:T(8,128)(2,1)S(1)} collective-permute-done((bf16[1024,256]{1,0:T(8,128)(2,1)}, bf16[1024,256]{1,0:T(8,128)(2,1)S(1)}, u32[]{:S(2)}, u32[]{:S(2)}) %collective-permute-start) | collective-permute-done | bytes 524320 | tf_op jit(solution)/shard_map/ppermute | solution.py:39
  148.7 5.6 %collective-permute-done.7 = bf16[1024,256]{1,0:T(8,128)(2,1)S(1)} collective-permute-done((bf16[1024,256]{1,0:T(8,128)(2,1)}, bf16[1024,256]{1,0:T(8,128)(2,1)S(1)}, u32[]{:S(2)}, u32[]{:S(2)}) %collective-permute-start.7) | collective-permute-done | bytes 524320 | tf_op jit(solution)/shard_map/ppermute | solution.py:39
  154.3 5.6 %collective-permute-done.1 = bf16[1024,256]{1,0:T(8,128)(2,1)S(1)} collective-permute-done((bf16[1024,256]{1,0:T(8,128)(2,1)S(1)}, bf16[1024,256]{1,0:T(8,128)(2,1)S(1)}, u32[]{:S(2)}, u32[]{:S(2)}) %collective-permute-start.1) | collective-permute-done | bytes 524320 | tf_op jit(solution)/shard_map/ppermute | solution.py:39
  160.0 5.6 %collective-permute-done.8 = bf16[1024,256]{1,0:T(8,128)(2,1)S(1)} collective-permute-done((bf16[1024,256]{1,0:T(8,128)(2,1)S(1)}, bf16[1024,256]{1,0:T(8,128)(2,1)S(1)}, u32[]{:S(2)}, u32[]{:S(2)}) %collective-permute-start.8) | collective-permute-done | bytes 524320 | tf_op jit(solution)/shard_map/ppermute | solution.py:39
  165.6 5.6 %collective-permute-done.2 = bf16[1024,256]{1,0:T(8,128)(2,1)S(1)} collective-permute-done((bf16[1024,256]{1,0:T(8,128)(2,1)S(1)}, bf16[1024,256]{1,0:T(8,128)(2,1)S(1)}, u32[]{:S(2)}, u32[]{:S(2)}) %collective-permute-start.2) | collective-permute-done | bytes 524320 | tf_op jit(solution)/shard_map/ppermute | solution.py:39
  171.2 5.7 %collective-permute-done.9 = bf16[1024,256]{1,0:T(8,128)(2,1)} collective-permute-done((bf16[1024,256]{1,0:T(8,128)(2,1)S(1)}, bf16[1024,256]{1,0:T(8,128)(2,1)}, u32[]{:S(2)}, u32[]{:S(2)}) %collective-permute-start.9) | collective-permute-done | bytes 524320 | tf_op jit(solution)/shard_map/ppermute | solution.py:39
  176.9 5.6 %collective-permute-done.3 = bf16[1024,256]{1,0:T(8,128)(2,1)} collective-permute-done((bf16[1024,256]{1,0:T(8,128)(2,1)S(1)}, bf16[1024,256]{1,0:T(8,128)(2,1)}, u32[]{:S(2)}, u32[]{:S(2)}) %collective-permute-start.3) | collective-permute-done | bytes 524320 | tf_op jit(solution)/shard_map/ppermute | solution.py:39
  183.4 4.7 %collective-permute-done.10 = bf16[1024,256]{1,0:T(8,128)(2,1)} collective-permute-done((bf16[1024,256]{1,0:T(8,128)(2,1)}, bf16[1024,256]{1,0:T(8,128)(2,1)}, u32[]{:S(2)}, u32[]{:S(2)}) %collective-permute-start.10) | collective-permute-done | bytes 524320 | tf_op jit(solution)/shard_map/ppermute | solution.py:39
  188.2 2.5 broadcast.21.clone.1
  191.6 2.5 %broadcast.21.clone = bf16[1024,2048]{1,0:T(8,128)(2,1)} broadcast(bf16[]{:T(256)} %constant.75.clone.1), dimensions={} | broadcast | bytes 4194306 | tf_op jit(solution)/shard_map/broadcast.3
  201.0 1.9 constant_dynamic-update-slice_fusion.4
  202.9 1.9 constant_dynamic-update-slice_fusion.11
  204.8 1.7 collective-permute-done.5
  206.5 1.9 constant_dynamic-update-slice_fusion.3
  208.4 3.7 %collective-permute-done.12 = bf16[1024,256]{1,0:T(8,128)(2,1)S(1)} collective-permute-done((bf16[1024,256]{1,0:T(8,128)(2,1)S(1)}, bf16[1024,256]{1,0:T(8,128)(2,1)S(1)}, u32[]{:S(2)}, u32[]{:S(2)}) %collective-permute-start.12) | collective-permute-done | bytes 524320 | tf_op jit(solution)/shard_map/ppermute | solution.py:39
  212.1 1.9 constant_dynamic-update-slice_fusion.10
  218.6 4.7 %collective-permute-done.13 = bf16[1024,256]{1,0:T(8,128)(2,1)S(1)} collective-permute-done((bf16[1024,256]{1,0:T(8,128)(2,1)S(1)}, bf16[1024,256]{1,0:T(8,128)(2,1)S(1)}, u32[]{:S(2)}, u32[]{:S(2)}) %collective-permute-start.13) | collective-permute-done | bytes 524320 | tf_op jit(solution)/shard_map/ppermute | solution.py:39
  224.2 10.7 %fusion = f32[512,1024]{1,0:T(8,128)} fusion(bf16[512,1024]{1,0:T(8,128)(2,1)} %get-tuple-element.5, bf16[1024,2048]{1,0:T(8,128)(2,1)} %constant_dynamic-update-slice_fusion, bf16[1024,2048]{1,0:T(8,128)(2,1)} %all-gather.2.cloned.1.call-done), kind=kOutput, calls=%fused_computation.1 | convolution fusion | flops 5369757696 | bytes 11534336 | tf_op jit(solution)/shard_map/dot_general | solution.py:43
  234.9 11.4 %add_multiply_fusion = f32[512,1024]{1,0:T(8,128)} fusion(f32[512,1024]{1,0:T(8,128)S(1)} %bitcast.17, f32[512,1024]{1,0:T(8,128)} %fusion, bf16[512,1024]{1,0:T(8,128)(2,1)} %get-tuple-element.7, bf16[1024,2048]{1,0:T(8,128)(2,1)} %constant_dynamic-update-slice_fusion.8, bf16[1024,2048]{1,0:T(8,128)(2,1)} %all-gather.2.cloned.1.call-done), kind=kOutput, calls=%fused_computation | convolution fusion | flops 5370806272 | bytes 15728640 | tf_op jit(solution)/shard_map/dot_general | solution.py:43
  (60 shorter events, 16.0 us)
Async XLA Ops:
  7.4 6.1 %copy-start = (bf16[512,1024]{1,0:T(8,128)(2,1)S(1)}, bf16[512,1024]{1,0:T(8,128)(2,1)}, u32[]{:S(2)}) copy-start(bf16[512,1024]{1,0:T(8,128)(2,1)} %param.4) | copy-start | bytes 3145732
  7.4 131.6 %all-reduce.3.cloned.1.call-start = ((), (), s32[]{:S(2)}) async-start(), calls=%async_computation.1 | async-start | bytes 6291456 | tf_op jit(solution)/shard_map/psum | solution.py:9
  15.0 209.2 %all-gather.2.cloned.1.call-start = ((), (), s32[]{:S(2)}) async-start(), calls=%async_computation | async-start | bytes 4718592 | tf_op jit(solution)/shard_map/all_gather | solution.py:29
  139.0 9.7 %collective-permute-start = (bf16[1024,256]{1,0:T(8,128)(2,1)}, bf16[1024,256]{1,0:T(8,128)(2,1)S(1)}, u32[]{:S(2)}, u32[]{:S(2)}) collective-permute-start(bf16[1024,256]{1,0:T(8,128)(2,1)} %get-tuple-element.8), channel_id=1, source_target_pairs={{0,4},{4,8},{8,12},{12,16},{16,20},{20,24},{24,28},{28,0},{1,5},{5... | collective-permute-start | bytes 1572872 | tf_op jit(solution)/shard_map/ppermute | solution.py:39
  139.0 15.3 %collective-permute-start.7 = (bf16[1024,256]{1,0:T(8,128)(2,1)}, bf16[1024,256]{1,0:T(8,128)(2,1)S(1)}, u32[]{:S(2)}, u32[]{:S(2)}) collective-permute-start(bf16[1024,256]{1,0:T(8,128)(2,1)} %get-tuple-element.6), channel_id=1, source_target_pairs={{0,4},{4,8},{8,12},{12,16},{16,20},{20,24},{24,28},{28,0},{1,5},{5... | collective-permute-start | bytes 1572872 | tf_op jit(solution)/shard_map/ppermute | solution.py:39
  148.7 11.2 %collective-permute-start.1 = (bf16[1024,256]{1,0:T(8,128)(2,1)S(1)}, bf16[1024,256]{1,0:T(8,128)(2,1)S(1)}, u32[]{:S(2)}, u32[]{:S(2)}) collective-permute-start(bf16[1024,256]{1,0:T(8,128)(2,1)S(1)} %collective-permute-done), channel_id=1, source_target_pairs={{0,4},{4,8},{8,12},{12,16},{16,20},{20,24},{24,28},{28,0},{1,5},{5... | collective-permute-start | bytes 1572872 | tf_op jit(solution)/shard_map/ppermute | solution.py:39
  154.3 28.2 %copy-start.9 = (bf16[1024,256]{1,0:T(8,128)(2,1)}, bf16[1024,256]{1,0:T(8,128)(2,1)S(1)}, u32[]{:S(2)}) copy-start(bf16[1024,256]{1,0:T(8,128)(2,1)S(1)} %collective-permute-done.7) | copy-start | bytes 1572868
  154.3 11.2 %collective-permute-start.8 = (bf16[1024,256]{1,0:T(8,128)(2,1)S(1)}, bf16[1024,256]{1,0:T(8,128)(2,1)S(1)}, u32[]{:S(2)}, u32[]{:S(2)}) collective-permute-start(bf16[1024,256]{1,0:T(8,128)(2,1)S(1)} %collective-permute-done.7), channel_id=1, source_target_pairs={{0,4},{4,8},{8,12},{12,16},{16,20},{20,24},{24,28},{28,0},{1,5},{5... | collective-permute-start | bytes 1572872 | tf_op jit(solution)/shard_map/ppermute | solution.py:39
  160.0 17.0 %copy-start.3 = (bf16[1024,256]{1,0:T(8,128)(2,1)}, bf16[1024,256]{1,0:T(8,128)(2,1)S(1)}, u32[]{:S(2)}) copy-start(bf16[1024,256]{1,0:T(8,128)(2,1)S(1)} %collective-permute-done.1) | copy-start | bytes 1572868
  160.0 11.2 %collective-permute-start.2 = (bf16[1024,256]{1,0:T(8,128)(2,1)S(1)}, bf16[1024,256]{1,0:T(8,128)(2,1)S(1)}, u32[]{:S(2)}, u32[]{:S(2)}) collective-permute-start(bf16[1024,256]{1,0:T(8,128)(2,1)S(1)} %collective-permute-done.1), channel_id=1, source_target_pairs={{0,4},{4,8},{8,12},{12,16},{16,20},{20,24},{24,28},{28,0},{1,5},{5... | collective-permute-start | bytes 1572872 | tf_op jit(solution)/shard_map/ppermute | solution.py:39
  165.6 11.3 %collective-permute-start.9 = (bf16[1024,256]{1,0:T(8,128)(2,1)S(1)}, bf16[1024,256]{1,0:T(8,128)(2,1)}, u32[]{:S(2)}, u32[]{:S(2)}) collective-permute-start(bf16[1024,256]{1,0:T(8,128)(2,1)S(1)} %collective-permute-done.8), channel_id=1, source_target_pairs={{0,4},{4,8},{8,12},{12,16},{16,20},{20,24},{24,28},{28,0},{1,5},{5... | collective-permute-start | bytes 1572872 | tf_op jit(solution)/shard_map/ppermute | solution.py:39
  171.2 5.7 %copy-start.5 = (bf16[1024,256]{1,0:T(8,128)(2,1)}, bf16[1024,256]{1,0:T(8,128)(2,1)S(1)}, u32[]{:S(2)}) copy-start(bf16[1024,256]{1,0:T(8,128)(2,1)S(1)} %collective-permute-done.2) | copy-start | bytes 1572868
  171.2 11.3 %collective-permute-start.3 = (bf16[1024,256]{1,0:T(8,128)(2,1)S(1)}, bf16[1024,256]{1,0:T(8,128)(2,1)}, u32[]{:S(2)}, u32[]{:S(2)}) collective-permute-start(bf16[1024,256]{1,0:T(8,128)(2,1)S(1)} %collective-permute-done.2), channel_id=1, source_target_pairs={{0,4},{4,8},{8,12},{12,16},{16,20},{20,24},{24,28},{28,0},{1,5},{5... | collective-permute-start | bytes 1572872 | tf_op jit(solution)/shard_map/ppermute | solution.py:39
  176.9 11.2 %collective-permute-start.10 = (bf16[1024,256]{1,0:T(8,128)(2,1)}, bf16[1024,256]{1,0:T(8,128)(2,1)}, u32[]{:S(2)}, u32[]{:S(2)}) collective-permute-start(bf16[1024,256]{1,0:T(8,128)(2,1)} %collective-permute-done.9), channel_id=1, source_target_pairs={{0,4},{4,8},{8,12},{12,16},{16,20},{20,24},{24,28},{28,0},{1,5},{5... | collective-permute-start | bytes 1572872 | tf_op jit(solution)/shard_map/ppermute | solution.py:39
  182.5 14.3 %collective-permute-start.4 = (bf16[1024,256]{1,0:T(8,128)(2,1)}, bf16[1024,256]{1,0:T(8,128)(2,1)}, u32[]{:S(2)}, u32[]{:S(2)}) collective-permute-start(bf16[1024,256]{1,0:T(8,128)(2,1)} %collective-permute-done.3), channel_id=1, source_target_pairs={{0,4},{4,8},{8,12},{12,16},{16,20},{20,24},{24,28},{28,0},{1,5},{5... | collective-permute-start | bytes 1572872 | tf_op jit(solution)/shard_map/ppermute | solution.py:39
  182.9 7.8 %copy-start.2 = (bf16[1024,256]{1,0:T(8,128)(2,1)S(1)}, bf16[1024,256]{1,0:T(8,128)(2,1)}, u32[]{:S(2)}) copy-start(bf16[1024,256]{1,0:T(8,128)(2,1)} %get-tuple-element.8) | copy-start | bytes 1572868
  183.4 10.7 %copy-start.1 = (bf16[1024,256]{1,0:T(8,128)(2,1)S(1)}, bf16[1024,256]{1,0:T(8,128)(2,1)}, u32[]{:S(2)}) copy-start(bf16[1024,256]{1,0:T(8,128)(2,1)} %get-tuple-element.6) | copy-start | bytes 1572868
  188.2 11.1 %collective-permute-start.11 = (bf16[1024,256]{1,0:T(8,128)(2,1)}, bf16[1024,256]{1,0:T(8,128)(2,1)S(1)}, u32[]{:S(2)}, u32[]{:S(2)}) collective-permute-start(bf16[1024,256]{1,0:T(8,128)(2,1)} %collective-permute-done.10), channel_id=1, source_target_pairs={{0,4},{4,8},{8,12},{12,16},{16,20},{20,24},{24,28},{28,0},{1,5},{5... | collective-permute-start | bytes 1572872 | tf_op jit(solution)/shard_map/ppermute | solution.py:39
  190.7 6.8 %copy-start.4 = (bf16[1024,256]{1,0:T(8,128)(2,1)S(1)}, bf16[1024,256]{1,0:T(8,128)(2,1)}, u32[]{:S(2)}) copy-start(bf16[1024,256]{1,0:T(8,128)(2,1)} %copy-done.3) | copy-start | bytes 1572868
  191.6 8.6 %copy-start.6 = (bf16[1024,256]{1,0:T(8,128)(2,1)S(1)}, bf16[1024,256]{1,0:T(8,128)(2,1)}, u32[]{:S(2)}) copy-start(bf16[1024,256]{1,0:T(8,128)(2,1)} %copy-done.5) | copy-start | bytes 1572868
  196.8 9.7 %collective-permute-start.5 = (bf16[1024,256]{1,0:T(8,128)(2,1)}, bf16[1024,256]{1,0:T(8,128)(2,1)S(1)}, u32[]{:S(2)}, u32[]{:S(2)}) collective-permute-start(bf16[1024,256]{1,0:T(8,128)(2,1)} %collective-permute-done.4), channel_id=1, source_target_pairs={{0,4},{4,8},{8,12},{12,16},{16,20},{20,24},{24,28},{28,0},{1,5},{5... | collective-permute-start | bytes 1572872 | tf_op jit(solution)/shard_map/ppermute | solution.py:39
  199.3 12.9 %collective-permute-start.12 = (bf16[1024,256]{1,0:T(8,128)(2,1)S(1)}, bf16[1024,256]{1,0:T(8,128)(2,1)S(1)}, u32[]{:S(2)}, u32[]{:S(2)}) collective-permute-start(bf16[1024,256]{1,0:T(8,128)(2,1)S(1)} %collective-permute-done.11), channel_id=1, source_target_pairs={{0,4},{4,8},{8,12},{12,16},{16,20},{20,24},{24,28},{28,0},{1,5},{5... | collective-permute-start | bytes 1572872 | tf_op jit(solution)/shard_map/ppermute | solution.py:39
  206.5 11.2 %collective-permute-start.6 = (bf16[1024,256]{1,0:T(8,128)(2,1)S(1)}, bf16[1024,256]{1,0:T(8,128)(2,1)S(1)}, u32[]{:S(2)}, u32[]{:S(2)}) collective-permute-start(bf16[1024,256]{1,0:T(8,128)(2,1)S(1)} %collective-permute-done.5), channel_id=1, source_target_pairs={{0,4},{4,8},{8,12},{12,16},{16,20},{20,24},{24,28},{28,0},{1,5},{5... | collective-permute-start | bytes 1572872 | tf_op jit(solution)/shard_map/ppermute | solution.py:39
  212.1 11.2 %collective-permute-start.13 = (bf16[1024,256]{1,0:T(8,128)(2,1)S(1)}, bf16[1024,256]{1,0:T(8,128)(2,1)S(1)}, u32[]{:S(2)}, u32[]{:S(2)}) collective-permute-start(bf16[1024,256]{1,0:T(8,128)(2,1)S(1)} %collective-permute-done.12), channel_id=1, source_target_pairs={{0,4},{4,8},{8,12},{12,16},{16,20},{20,24},{24,28},{28,0},{1,5},{5... | collective-permute-start | bytes 1572872 | tf_op jit(solution)/shard_map/ppermute | solution.py:39
  (3 other events, 15.2 us)
Sparse Core Ops, SparseCore 0:
  15.2 123.8 all-reduce.2
Sparse Core Ops, SparseCore 1:
  17.4 39.9 all-gather.1
